TPU v7x, 32 devices: a whole 2x2x4 slice. The times are simulated.
32 devices in a mesh: group: 16 (over z, y, core), tp: 2 (over x).
Axes of the slice: x: 2, y: 2, z: 4, core: 2. Of those that a mesh axis runs over, the one named last changes fastest.
Arguments:
- tokens: bfloat16 [8192, 3200], P('group', 'tp'), may hold values from -6 to 6
- norm_gain: bfloat16 [3200], P('tp'), may hold values from 0.25 to 1.75
- w_qkv: bfloat16 [3200, 3, 2048], P('group', None, 'tp'), may hold values from -1 to 1, as said below
- qk_gain: float32 [2, 2048], P(None, 'tp'), may hold values from 0.5 to 8
- w_out: bfloat16 [2048, 3200], P('tp', 'group'), may hold values from -0.125 to 0.125
- layer_scale: float32 [3200], P('tp'), may hold values from 0.3 to 1.5
- request: int32 [8192], P('group'), may hold values from 0 to 8191, as said below
- owner: int32 [8192, 1], P('group'), may hold values from 0 to 15; in each aligned block of 512 rows (0 to 511, 512 to 1023, ...) at most 64 rows name the same one
Outputs:
- routed: bfloat16 [16, 16, 64, 3200], P('group', None, None, 'tp')
Inputs may be any that keep to these rules, and one draw needn't show every extreme that they name: Requests never cross a block of 1024 rows starting at a multiple of 1024, and blocks share none; in each such block exactly one request holds rows on both sides of its middle, at most 128 on each side, exactly 128 on each side in the first block; the first row's number is 0 and the last row's is 8191. Among one group's 512 rows at most 64 name the same owner; some owner is named by exactly 64 rows of some group. `w_qkv`: column scales of the projections vary across the columns.
All inputs are finite; a program needn't handle non-finite values.
Results may differ from a plain program's by a relative error of at most 0.0117.
The roundings to bfloat16 on the way count: a program that leaves them out, or rounds other values in their place, can miss the bound.
Values may be sent and summed in bfloat16 or wider, within the bound.
A program may use at most 128 MiB of HBM per device.

v0:
```python
import math
import jax
import jax.numpy as jnp
from jax import lax
from jax.sharding import PartitionSpec as P

HD = 128
SHARE = 128


def swapped(value, axis, apart):
    mask = 2**apart
    pairs = [(source, source ^ mask) for source in range(lax.axis_size(axis))]
    return lax.ppermute(value, axis, pairs)


def from_next(value, axis):
    count = lax.axis_size(axis)
    return lax.ppermute(value, axis, [((i + 1) % count, i) for i in range(count)])


def shards(tokens, norm_gain, w_qkv, qk_gain, w_out, layer_scale, request, owner):
    rows, feat_local = tokens.shape
    tp_count = lax.axis_size("tp")
    group_count = lax.axis_size("group")
    local_width = w_qkv.shape[2]
    head_count = local_width // HD
    me_tp = lax.axis_index("tp")
    w_all = lax.all_gather(
        w_qkv.reshape(w_qkv.shape[0], 3 * local_width), "group", axis=0, tiled=True
    )
    whole = jnp.zeros((rows, feat_local * tp_count), jnp.bfloat16)
    gain_all = jnp.zeros((1, feat_local * tp_count), jnp.bfloat16)
    piece, gain = (tokens, norm_gain.reshape(1, feat_local))
    for step in range(tp_count):
        at = (me_tp + step) % tp_count * feat_local
        whole = lax.dynamic_update_slice(whole, piece, (0, at))
        gain_all = lax.dynamic_update_slice(gain_all, gain, (0, at))
        if step < tp_count - 1:
            piece, gain = (from_next(piece, "tp"), from_next(gain, "tp"))
    whole, late_out = lax.optimization_barrier((whole, w_out))
    per = group_count // tp_count
    pairs = []
    for g in range(group_count):
        for b in range(tp_count):
            t, j = (g // per, g % per)
            to_g = (b - t) % tp_count * per + j
            pairs.append((g * tp_count + b, to_g * tp_count + t))
    w_piece = lax.ppermute(late_out.T, ("group", "tp"), pairs)
    w_o = lax.all_gather(w_piece, "group", axis=0, tiled=True)
    w_o = w_o.reshape(tp_count, feat_local, local_width)
    xwide = whole.astype(jnp.float32)
    stat = jnp.mean(xwide * xwide, axis=-1, keepdims=True)
    normed = (xwide * lax.rsqrt(stat + 1e-06) * gain_all.astype(jnp.float32)).astype(jnp.bfloat16)
    qkv = jnp.dot(normed, w_all, preferred_element_type=jnp.float32)
    query = qkv[:, :local_width]
    key_rows = qkv[:, local_width : 2 * local_width]
    value = qkv[:, 2 * local_width :].astype(jnp.bfloat16)
    qsum, ksum = lax.psum(
        (jnp.sum(query * query, axis=-1), jnp.sum(key_rows * key_rows, axis=-1)), "tp"
    )
    total_width = local_width * tp_count
    qnorm = (query * lax.rsqrt(qsum / total_width + 1e-06)[:, None] * qk_gain[0]).astype(
        jnp.bfloat16
    )
    knorm = (key_rows * lax.rsqrt(ksum / total_width + 1e-06)[:, None] * qk_gain[1]).astype(
        jnp.bfloat16
    )
    parity = lax.axis_index("group") % 2
    seam = jnp.where(parity == 0, rows - SHARE, 0).astype(jnp.int32)
    key_window = lax.dynamic_slice_in_dim(knorm, seam, SHARE, 0)
    id_window = lax.dynamic_slice_in_dim(request, seam, SHARE, 0)
    paired_key, paired_ids = swapped((key_window, id_window), "group", 0)
    all_keys = jnp.concatenate([knorm, paired_key], axis=0)
    all_ids = jnp.concatenate([request, paired_ids], axis=0)
    qheads = qnorm.reshape(rows, head_count, HD)
    kheads = all_keys.reshape(rows + SHARE, head_count, HD)
    scores = jnp.einsum(
        "qhd,khd->hqk", qheads, kheads, preferred_element_type=jnp.float32
    ) / math.sqrt(HD)
    same = request[:, None] == all_ids[None, :]
    scores = jnp.where(same[None], scores, -jnp.inf)
    top = jnp.max(scores, axis=-1, keepdims=True)
    expo = jnp.exp(scores - top)
    probs = (expo / jnp.sum(expo, axis=-1, keepdims=True)).astype(jnp.bfloat16)
    value_window = lax.dynamic_slice_in_dim(value, seam, SHARE, 0)
    all_values = jnp.concatenate([value, swapped(value_window, "group", 0)], axis=0)
    vheads = all_values.reshape(rows + SHARE, head_count, HD)
    attended = jnp.einsum("hqk,khd->qhd", probs, vheads, preferred_element_type=jnp.float32)
    attended = attended.astype(jnp.bfloat16).reshape(rows, local_width)
    branch = jnp.zeros((rows, feat_local), jnp.float32)
    for step in range(tp_count):
        onward = from_next(attended, "tp") if step < tp_count - 1 else None
        part = lax.dot_general(
            attended, w_o[step], (((1,), (1,)), ((), ())), preferred_element_type=jnp.float32
        )
        branch = branch + part.astype(jnp.bfloat16).astype(jnp.float32)
        attended = onward
    mixed = (tokens.astype(jnp.float32) + layer_scale * branch).astype(jnp.bfloat16)
    capacity = max(2, 2 * rows // group_count)
    target = owner[:, 0]
    onehot = (target[:, None] == jnp.arange(group_count, dtype=jnp.int32)[None, :]).astype(
        jnp.int32
    )
    slot = jnp.sum((jnp.cumsum(onehot, axis=0) - onehot) * onehot, axis=-1)
    place = target * capacity + slot
    select = (
        jnp.arange(group_count * capacity, dtype=jnp.int32)[:, None] == place[None, :]
    ).astype(jnp.bfloat16)
    outbox = jnp.dot(select, mixed, preferred_element_type=jnp.float32).astype(jnp.bfloat16)
    outbox = outbox.reshape(group_count, capacity, feat_local)
    inbox = lax.all_to_all(outbox, "group", split_axis=0, concat_axis=0, tiled=True)
    return inbox[None]


def solution(mesh):
    in_specs = (
        P("group", "tp"),
        P("tp"),
        P("group", None, "tp"),
        P(None, "tp"),
        P("tp", "group"),
        P("tp"),
        P("group"),
        P("group", None),
    )
    out_specs = P("group", None, None, "tp")
    return jax.shard_map(shards, mesh=mesh, in_specs=in_specs, out_specs=out_specs, check_vma=False)
```

profile of v0, /device:TPU:1, one launch (start us, length us, event | category | flops | bytes accessed | tf_op | source)
XLA Modules:
  0.0 316.9 jit_solution(11441685035728626753)
XLA Ops:
  6.5 2.4 copy.23
  9.0 2.1 collective-permute-start
  11.4 1.6 constant_dynamic-update-slice_fusion.1
  13.0 33.9 %collective-permute-done = bf16[512,1600]{0,1:T(8,128)(2,1)} collective-permute-done((bf16[512,1600]{0,1:T(8,128)(2,1)}, bf16[512,1600]{0,1:T(8,128)(2,1)}, u32[]{:S(2)}, u32[]{:S(2)}) %collective-permute-start) | collective-permute-done | bytes 1638432 | tf_op jit(solution)/shard_map/ppermute | solution.py:19
  47.0 1.6 constant_dynamic-update-slice_fusion
  50.1 31.1 %collective-permute-start.1 = (bf16[1,1600]{1,0:T(2,128)(2,1)S(1)}, bf16[1,1600]{1,0:T(2,128)(2,1)S(1)}, u32[]{:S(2)}, u32[]{:S(2)}) collective-permute-start(bf16[1,1600]{1,0:T(2,128)(2,1)S(1)} %reshape.96), channel_id=1, source_target_pairs={{1,0},{0,1},{3,2},{2,3},{5,4},{4,5},{7,6},{6,7},{9,8},{8,9},{11,10... | collective-permute-start | bytes 9608 | tf_op jit(solution)/shard_map/ppermute | solution.py:19
  81.3 2.3 collective-permute-start.3
  85.5 28.8 %all-gather.3.cloned.1.call-done = bf16[3200,3072]{1,0:T(8,128)(2,1)} async-done(((bf16[200,3072]{1,0:T(8,128)(2,1)}), bf16[3200,3072]{1,0:T(8,128)(2,1)}) %all-gather.3.cloned.1.call-update) | async-done | bytes 19660816 | tf_op jit(solution)/shard_map/all_gather | solution.py:29
  114.3 14.3 %fusion.9 = f32[512,3072]{1,0:T(8,128)S(1)} fusion(bf16[3200,3072]{1,0:T(8,128)(2,1)} %all-gather.3.cloned.1.call-done, bf16[512,3200]{0,1:T(8,128)(2,1)S(1)} %constant_dynamic-update-slice_fusion, f32[3200]{0:T(1024)S(1)} %mul.106, f32[512]{0:T(512)S(1)} %add_rsqrt_fusion.2), kind=kOutput, calls=%fused_computation.15 | convolution fusion | flops 10072883200 | bytes 29243904 | tf_op jit(solution)/shard_map/dot_general | solution.py:55
  129.5 1.8 copy-done
  131.3 14.3 %all-reduce = (f32[512]{0:T(512)S(1)}, f32[512]{0:T(512)S(1)}) all-reduce(f32[512]{0:T(512)S(1)} %get-tuple-element.10, f32[512]{0:T(512)S(1)} %get-tuple-element.9), channel_id=1, replica_groups=mesh['group'=16,'tp'=2] {'tp'}, use_global_device_ids=true, to_apply=%region_7.8 | all-reduce | flops 1024 | bytes 8192 | tf_op jit(solution)/shard_map/psum | solution.py:59
  145.6 3.7 %fusion.29 = (bf16[64,8,8,128]{3,2,1,0:T(8,128)(2,1)}, bf16[512,1024]{1,0:T(8,128)(2,1)S(1)}) fusion(f32[512,3072]{1,0:T(8,128)} %copy-done, f32[1024]{0:T(1024)S(1)} %bitcast.56, f32[512]{0:T(512)S(1)} %get-tuple-element.20, f32[1024]{0:T(1024)S(1)} %bitcast.57, f32[512]{0:T(512)S(1)} %get-tuple-element.19), kind=kLoop, calls=%fused_computation.37 | loop fusion | flops 3145728 | bytes 6303744
  152.8 1.4 copy.19
  154.2 6.5 %fusion.26 = f32[8,512,640]{2,1,0:T(8,128)} fusion(bf16[64,8,8,128]{3,2,1,0:T(8,128)(2,1)S(1)} %copy-done.1, bf16[128,1024]{1,0:T(8,128)(2,1)} %collective-permute-done.4, bf16[512,1024]{1,0:T(8,128)(2,1)S(1)} %get-tuple-element.14), kind=kOutput, calls=%fused_computation.32 | convolution fusion | flops 673710080 | bytes 12845056 | tf_op jit(solution)/shard_map/qhd,khd->hqk/dot_general | solution.py:78
  160.8 16.0 %fusion.42 = (f32[8,512]{1,0:T(8,128)S(1)}, f32[8,512,640]{2,1,0:T(8,128)}) fusion(f32[8,512,640]{2,1,0:T(8,128)} %fusion.26, pred[512,640]{1,0:T(8,128)(4,1)S(1)} %copy-done.3), kind=kOutput, calls=%fused_computation.63 | output fusion | flops 15729279 | bytes 21315584 | tf_op jit(solution)/shard_map/sub | solution.py:84
  176.8 6.0 %fusion.25 = bf16[8,128,512]{2,1,0:T(8,128)(2,1)S(1)} fusion(bf16[640,8,128]{0,2,1:T(8,128)(2,1)S(1)} %bitcast.51, f32[8,512,640]{2,1,0:T(8,128)} %get-tuple-element.18, f32[8,512]{1,0:T(8,128)S(1)} %get-tuple-element.17), kind=kOutput, calls=%fused_computation.31 | convolution fusion | flops 676855808 | bytes 12861440 | tf_op jit(solution)/shard_map/hqk,khd->qhd/dot_general | solution.py:89
  182.8 1.8 collective-permute-start.6
  186.3 10.2 %all-gather.5.cloned.1.call-done = bf16[3200,1024]{1,0:T(8,128)(2,1)} async-done(((bf16[200,1024]{1,0:T(8,128)(2,1)}), bf16[3200,1024]{1,0:T(8,128)(2,1)}) %all-gather.5.cloned.1.call-update) | async-done | bytes 6553616 | tf_op jit(solution)/shard_map/all_gather | solution.py:50
  196.6 5.0 %fusion.17 = bf16[512,1600]{0,1:T(8,128)(2,1)} fusion(bf16[512,1024]{0,1:T(8,128)(2,1)S(1)} %bitcast.59, bf16[3200,1024]{1,0:T(8,128)(2,1)} %all-gather.5.cloned.1.call-done), kind=kOutput, calls=%fused_computation.23 | convolution fusion | flops 1678540800 | bytes 5963776 | tf_op jit(solution)/shard_map/dot_general | solution.py:94
  201.6 6.6 %collective-permute-done.6 = bf16[512,1024]{0,1:T(8,128)(2,1)S(1)} collective-permute-done((bf16[512,1024]{0,1:T(8,128)(2,1)S(1)}, bf16[512,1024]{0,1:T(8,128)(2,1)S(1)}, u32[]{:S(2)}, u32[]{:S(2)}) %collective-permute-start.6) | collective-permute-done | bytes 1048608 | tf_op jit(solution)/shard_map/ppermute | solution.py:19
  208.2 8.5 %convolution_convert_fusion = bf16[1024,1600]{0,1:T(8,128)(2,1)} fusion(s32[512]{0:T(512)S(1)} %multiply_add_fusion, bf16[512,1600]{0,1:T(8,128)(2,1)} %fusion.17, bf16[512,1600]{0,1:T(8,128)(2,1)} %param.8, bf16[512,1024]{0,1:T(8,128)(2,1)S(1)} %collective-permute-done.6, bf16[3200,1024]{1,0:T(8,128)(2,1)} %all-gather.5.cloned.1.call-done, ...), kind=kOutput, calls=%fused_computation.14 | convolution fusion | flops 3364159488 | bytes 10887424 | tf_op jit(solution)/shard_map/dot_general | solution.py:110
  216.7 4.3 %copy.18 = bf16[1024,1600]{1,0:T(8,128)(2,1)S(1)} copy(bf16[1024,1600]{0,1:T(8,128)(2,1)} %convolution_convert_fusion) | data formatting | bytes 6553600 | tf_op jit(solution)/shard_map/convert_element_type | solution.py:110
  221.1 87.3 %all_to_all.5 = bf16[16,64,1600]{2,1,0:T(8,128)(2,1)S(1)} all-to-all(bf16[16,64,1600]{2,1,0:T(8,128)(2,1)S(1)} %bitcast.48), channel_id=1, replica_groups=mesh['group'=16,'tp'=2] {'group'}, dimensions={0} | all-to-all | bytes 6553600 | tf_op jit(solution)/shard_map/all_to_all | solution.py:112
  308.3 1.8 copy.38
  (57 shorter events, 9.8 us)
Async XLA Ops:
  6.5 107.8 %all-gather.3.cloned.1.call-start = ((), (), s32[]{:S(2)}) async-start(), calls=%async_computation.1 | async-start | bytes 20889600 | tf_op jit(solution)/shard_map/all_gather | solution.py:29
  9.0 187.6 %all-gather.5.cloned.1.call-start = ((), (), s32[]{:S(2)}) async-start(), calls=%async_computation.2 | async-start | bytes 6963200 | tf_op jit(solution)/shard_map/all_gather | solution.py:50
  9.0 38.0 %collective-permute-start = (bf16[512,1600]{0,1:T(8,128)(2,1)}, bf16[512,1600]{0,1:T(8,128)(2,1)}, u32[]{:S(2)}, u32[]{:S(2)}) collective-permute-start(bf16[512,1600]{0,1:T(8,128)(2,1)} %param.8), channel_id=1, source_target_pairs={{1,0},{0,1},{3,2},{2,3},{5,4},{4,5},{7,6},{6,7},{9,8},{8,9},{11,10... | collective-permute-start | bytes 4915208 | tf_op jit(solution)/shard_map/ppermute | solution.py:19
  11.3 37.2 %copy-start.8 = (bf16[1024,200]{0,1:T(8,128)(2,1)S(1)}, bf16[1024,200]{0,1:T(8,128)(2,1)}, u32[]{:S(2)}) copy-start(bf16[1024,200]{0,1:T(8,128)(2,1)} %param.12) | copy-start | bytes 1228804
  11.3 38.7 %copy-start.5 = (bf16[1600]{0:T(1024)(128)(2,1)S(1)}, bf16[1600]{0:T(1024)(128)(2,1)}, u32[]{:S(2)}) copy-start(bf16[1600]{0:T(1024)(128)(2,1)} %param.9) | copy-start | bytes 9604
  11.4 69.8 %copy-start.6 = (s32[512]{0:T(512)S(1)}, s32[512]{0:T(512)}, u32[]{:S(2)}) copy-start(s32[512]{0:T(512)} %param.14) | copy-start | bytes 6148
  11.4 72.2 %copy-start.7 = (f32[2,1024]{1,0:T(2,128)S(1)}, f32[2,1024]{1,0:T(2,128)}, u32[]{:S(2)}) copy-start(f32[2,1024]{1,0:T(2,128)} %param.11) | copy-start | bytes 24580
  48.6 1.4 collective-permute-start.5
  50.1 34.4 %collective-permute-start.1 = (bf16[1,1600]{1,0:T(2,128)(2,1)S(1)}, bf16[1,1600]{1,0:T(2,128)(2,1)S(1)}, u32[]{:S(2)}, u32[]{:S(2)}) collective-permute-start(bf16[1,1600]{1,0:T(2,128)(2,1)S(1)} %reshape.96), channel_id=1, source_target_pairs={{1,0},{0,1},{3,2},{2,3},{5,4},{4,5},{7,6},{6,7},{9,8},{8,9},{11,10... | collective-permute-start | bytes 9608 | tf_op jit(solution)/shard_map/ppermute | solution.py:19
  81.3 3.2 collective-permute-start.3
  128.6 2.7 copy-start
  128.8 22.9 %collective-permute-start.2 = (bf16[128,1024]{1,0:T(8,128)(2,1)S(1)}, bf16[128,1024]{1,0:T(8,128)(2,1)}, u32[]{:S(2)}, u32[]{:S(2)}) collective-permute-start(bf16[128,1024]{1,0:T(8,128)(2,1)S(1)} %constant_dynamic-slice_fusion.1), channel_id=1, source_target_pairs={{0,2},{2,0},{4,6},{6,4},{8,10},{10,8},{12,14},{14,12},{16,18},{18,... | collective-permute-start | bytes 786440 | tf_op jit(solution)/shard_map/ppermute | solution.py:14
  150.0 4.2 %collective-permute-start.4 = (bf16[128,1024]{1,0:T(8,128)(2,1)}, bf16[128,1024]{1,0:T(8,128)(2,1)}, u32[]{:S(2)}, u32[]{:S(2)}) collective-permute-start(bf16[128,1024]{1,0:T(8,128)(2,1)} %constant_dynamic-slice_fusion), channel_id=1, source_target_pairs={{0,2},{2,0},{4,6},{6,4},{8,10},{10,8},{12,14},{14,12},{16,18},{18,... | collective-permute-start | bytes 786440 | tf_op jit(solution)/shard_map/ppermute | solution.py:14
  152.8 1.5 copy-start.1
  154.2 6.5 %copy-start.3 = (pred[512,640]{1,0:T(8,128)(4,1)S(1)}, pred[512,640]{1,0:T(8,128)(4,1)}, u32[]{:S(2)}) copy-start(pred[512,640]{1,0:T(8,128)(4,1)} %broadcast_compare_fusion) | copy-start | bytes 983044
  160.8 16.0 %copy-start.2 = (bf16[640,1024]{0,1:T(8,128)(2,1)S(1)}, bf16[640,1024]{0,1:T(8,128)(2,1)}, u32[]{:S(2)}) copy-start(bf16[640,1024]{0,1:T(8,128)(2,1)} %copy.19) | copy-start | bytes 3932164
  176.8 7.8 %copy-start.4 = (s32[512,1]{0,1:T(1,128)S(1)}, s32[512,1]{0,1:T(1,128)}, u32[]{:S(2)}) copy-start(s32[512,1]{0,1:T(1,128)} %param.15) | copy-start | bytes 6148
  182.8 25.4 %collective-permute-start.6 = (bf16[512,1024]{0,1:T(8,128)(2,1)S(1)}, bf16[512,1024]{0,1:T(8,128)(2,1)S(1)}, u32[]{:S(2)}, u32[]{:S(2)}) collective-permute-start(bf16[512,1024]{0,1:T(8,128)(2,1)S(1)} %bitcast.58), channel_id=1, source_target_pairs={{1,0},{0,1},{3,2},{2,3},{5,4},{4,5},{7,6},{6,7},{9,8},{8,9},{11,10... | collective-permute-start | bytes 3145736 | tf_op jit(solution)/shard_map/ppermute | solution.py:19
  186.3 21.9 %copy-start.9 = (f32[1600]{0:T(1024)S(1)}, f32[1600]{0:T(1024)}, u32[]{:S(2)}) copy-start(f32[1600]{0:T(1024)} %param.13) | copy-start | bytes 19204
Sparse Core Ops, SparseCore 0:
  9.1 105.1 all-gather.2
  116.6 79.9 all-gather.4
where the time goes:
time: 317 us
  blocking collectives  102 us (32%)
  waiting for transfers between devices  80.1 us (25%)
  matrix products  40.3 us (13%)
  starting transfers between devices  39.9 us (13%)
  other arithmetic  24.4 us (8%)
  local copies, waits for them, and re-layouts  17 us (5%)
  between operations  13.6 us (4%)
    all_to_all x1, blocking collectives, shards(): lax.all_to_all(outbox, 'group', split_axis=0, concat_axis=0, tiled=True)  87.3 us
    ppermute x3, waiting for transfers between devices, from_next(): lax.ppermute(value, axis, [((i + 1) % count, i) for i in range(count)])  40.6 us
    ppermute x3, starting transfers between devices, from_next(): lax.ppermute(value, axis, [((i + 1) % count, i) for i in range(count)])  35.1 us
    all_gather x1, waiting for transfers between devices, shards(): lax.all_gather(w_qkv.reshape(w_qkv.shape[0], 3 * local_width), 'group', a...  28.8 us
    sub x1, other arithmetic, shards(): expo = jnp.exp(scores - top)  16 us
    psum x1, blocking collectives, shards(): lax.psum((jnp.sum(query * query, axis=-1), jnp.sum(key_rows * key_rows, a...  14.3 us
    dot_general x1, matrix products, shards(): qkv = jnp.dot(normed, w_all, preferred_element_type=jnp.float32)  14.3 us
    all_gather x1, waiting for transfers between devices, shards(): w_o = lax.all_gather(w_piece, 'group', axis=0, tiled=True)  10.2 us
  transfers between devices with their start and end apart: 9, of which 5 were waited for; matrix products, arithmetic and copies ran while one was open for 20% of the time, Pallas kernels for 0%

commit v1 on v0

--- a/solution.py
+++ b/solution.py
@@ -47,7 +47,14 @@
             to_g = (b - t) % tp_count * per + j
             pairs.append((g * tp_count + b, to_g * tp_count + t))
     w_piece = lax.ppermute(late_out.T, ("group", "tp"), pairs)
-    w_o = lax.all_gather(w_piece, "group", axis=0, tiled=True)
+    ring = [w_piece]
+    for hop in range(15):
+        ring.append(lax.ppermute(ring[-1], "group", [(dev, (dev + 1) % 16) for dev in range(16)]))
+    w_o = jnp.roll(
+        jnp.concatenate(ring[::-1], axis=0),
+        (lax.axis_index("group") + 1) * ring[0].shape[0],
+        axis=0,
+    )
     w_o = w_o.reshape(tp_count, feat_local, local_width)
     xwide = whole.astype(jnp.float32)
     stat = jnp.mean(xwide * xwide, axis=-1, keepdims=True)

time: 317 us -> 483 us (1.52)
  waiting for transfers between devices: 80.1 us -> 209 us
  local copies, waits for them, and re-layouts: 17 us -> 63.3 us
  blocking collectives: 102 us -> 89.7 us
    ppermute x0 -> x15, waiting for transfers between devices: none -> 161 us  [shards(): lax.ppermute(ring[-1], 'group', [(dev, (dev + 1) % 16) for dev in range(1...]
    unnamed x21 -> x106, local copies, waits for them, and re-layouts: 3.59 us -> 49.2 us
    all_gather x1, waiting for transfers between devices: 28.8 us -> 0.01 us  [shards(): lax.all_gather(w_qkv.reshape(w_qkv.shape[0], 3 * local_width), 'group', a...]
    ppermute x3, starting transfers between devices: 35.1 us -> 11.5 us  [from_next(): lax.ppermute(value, axis, [((i + 1) % count, i) for i in range(count)])]
    ppermute x3, starting transfers between devices: 3.36 us -> 18.9 us  [swapped(): return lax.ppermute(value, axis, pairs)]
    all_gather x1 -> x0, waiting for transfers between devices: 10.2 us -> none  [shards(): w_o = lax.all_gather(w_piece, 'group', axis=0, tiled=True)]
    ppermute x0 -> x15, starting transfers between devices: none -> 9.84 us  [shards(): lax.ppermute(ring[-1], 'group', [(dev, (dev + 1) % 16) for dev in range(1...]
    all_to_all x1, blocking collectives: 87.3 us -> 79.9 us  [shards(): lax.all_to_all(outbox, 'group', split_axis=0, concat_axis=0, tiled=True)]
  transfers between devices with their start and end apart: 9 -> 23, of which waited for: 5 -> 16; matrix products, arithmetic and copies ran while one was open for 20% -> 12% of each run, Pallas kernels for 0% -> 0%
where the time goes in v1:
time: 483 us
  waiting for transfers between devices  209 us (43%)
  blocking collectives  89.7 us (19%)
  local copies, waits for them, and re-layouts  63.3 us (13%)
  starting transfers between devices  41.9 us (9%)
  matrix products  40.9 us (8%)
  other arithmetic  23.6 us (5%)
  between operations  13.7 us (3%)
    ppermute x15, waiting for transfers between devices, shards(): lax.ppermute(ring[-1], 'group', [(dev, (dev + 1) % 16) for dev in range(1...  161 us
    all_to_all x1, blocking collectives, shards(): lax.all_to_all(outbox, 'group', split_axis=0, concat_axis=0, tiled=True)  79.9 us
    unnamed x106, local copies, waits for them, and re-layouts  49.2 us
    ppermute x3, waiting for transfers between devices, from_next(): lax.ppermute(value, axis, [((i + 1) % count, i) for i in range(count)])  47.9 us
    ppermute x3, starting transfers between devices, swapped(): return lax.ppermute(value, axis, pairs)  18.9 us
    sub x1, other arithmetic, shards(): expo = jnp.exp(scores - top)  15.5 us
    dot_general x1, matrix products, shards(): qkv = jnp.dot(normed, w_all, preferred_element_type=jnp.float32)  14.3 us
    ppermute x3, starting transfers between devices, from_next(): lax.ppermute(value, axis, [((i + 1) % count, i) for i in range(count)])  11.5 us
  transfers between devices with their start and end apart: 23, of which 16 were waited for; matrix products, arithmetic and copies ran while one was open for 12% of the time, Pallas kernels for 0%

profile of v1, /device:TPU:1, one launch (start us, length us, event | category | flops | bytes accessed | tf_op | source)
XLA Modules:
  0.0 482.5 jit_solution(7151782634676789641)
XLA Ops:
  12.9 34.0 %collective-permute-done = bf16[512,1600]{0,1:T(8,128)(2,1)} collective-permute-done((bf16[512,1600]{0,1:T(8,128)(2,1)}, bf16[512,1600]{0,1:T(8,128)(2,1)}, u32[]{:S(2)}, u32[]{:S(2)}) %collective-permute-start) | collective-permute-done | bytes 1638432 | tf_op jit(solution)/shard_map/ppermute | solution.py:19
  53.7 13.6 %collective-permute-done.6 = bf16[200,1024]{1,0:T(8,128)(2,1)S(1)} collective-permute-done((bf16[200,1024]{1,0:T(8,128)(2,1)S(1)}, bf16[200,1024]{1,0:T(8,128)(2,1)S(1)}, u32[]{:S(2)}, u32[]{:S(2)}) %collective-permute-start.6) | collective-permute-done | bytes 409632 | tf_op jit(solution)/shard_map/ppermute | solution.py:52
  70.5 32.5 %collective-permute-done.7 = bf16[200,1024]{1,0:T(8,128)(2,1)S(1)} collective-permute-done((bf16[200,1024]{1,0:T(8,128)(2,1)S(1)}, bf16[200,1024]{1,0:T(8,128)(2,1)S(1)}, u32[]{:S(2)}, u32[]{:S(2)}) %collective-permute-start.7) | collective-permute-done | bytes 409632 | tf_op jit(solution)/shard_map/ppermute | solution.py:52
  103.7 18.6 %collective-permute-done.8 = bf16[200,1024]{1,0:T(8,128)(2,1)S(1)} collective-permute-done((bf16[200,1024]{1,0:T(8,128)(2,1)S(1)}, bf16[200,1024]{1,0:T(8,128)(2,1)S(1)}, u32[]{:S(2)}, u32[]{:S(2)}) %collective-permute-start.8) | collective-permute-done | bytes 409632 | tf_op jit(solution)/shard_map/ppermute | solution.py:52
  123.1 10.1 %collective-permute-done.9 = bf16[200,1024]{1,0:T(8,128)(2,1)S(1)} collective-permute-done((bf16[200,1024]{1,0:T(8,128)(2,1)S(1)}, bf16[200,1024]{1,0:T(8,128)(2,1)S(1)}, u32[]{:S(2)}, u32[]{:S(2)}) %collective-permute-start.9) | collective-permute-done | bytes 409632 | tf_op jit(solution)/shard_map/ppermute | solution.py:52
  134.0 10.1 %collective-permute-done.10 = bf16[200,1024]{1,0:T(8,128)(2,1)S(1)} collective-permute-done((bf16[200,1024]{1,0:T(8,128)(2,1)S(1)}, bf16[200,1024]{1,0:T(8,128)(2,1)S(1)}, u32[]{:S(2)}, u32[]{:S(2)}) %collective-permute-start.10) | collective-permute-done | bytes 409632 | tf_op jit(solution)/shard_map/ppermute | solution.py:52
  144.8 10.1 %collective-permute-done.11 = bf16[200,1024]{1,0:T(8,128)(2,1)S(1)} collective-permute-done((bf16[200,1024]{1,0:T(8,128)(2,1)S(1)}, bf16[200,1024]{1,0:T(8,128)(2,1)S(1)}, u32[]{:S(2)}, u32[]{:S(2)}) %collective-permute-start.11) | collective-permute-done | bytes 409632 | tf_op jit(solution)/shard_map/ppermute | solution.py:52
  155.6 10.1 %collective-permute-done.12 = bf16[200,1024]{1,0:T(8,128)(2,1)S(1)} collective-permute-done((bf16[200,1024]{1,0:T(8,128)(2,1)S(1)}, bf16[200,1024]{1,0:T(8,128)(2,1)S(1)}, u32[]{:S(2)}, u32[]{:S(2)}) %collective-permute-start.12) | collective-permute-done | bytes 409632 | tf_op jit(solution)/shard_map/ppermute | solution.py:52
  166.5 10.1 %collective-permute-done.13 = bf16[200,1024]{1,0:T(8,128)(2,1)S(1)} collective-permute-done((bf16[200,1024]{1,0:T(8,128)(2,1)S(1)}, bf16[200,1024]{1,0:T(8,128)(2,1)S(1)}, u32[]{:S(2)}, u32[]{:S(2)}) %collective-permute-start.13) | collective-permute-done | bytes 409632 | tf_op jit(solution)/shard_map/ppermute | solution.py:52
  177.3 10.1 %collective-permute-done.14 = bf16[200,1024]{1,0:T(8,128)(2,1)S(1)} collective-permute-done((bf16[200,1024]{1,0:T(8,128)(2,1)S(1)}, bf16[200,1024]{1,0:T(8,128)(2,1)S(1)}, u32[]{:S(2)}, u32[]{:S(2)}) %collective-permute-start.14) | collective-permute-done | bytes 409632 | tf_op jit(solution)/shard_map/ppermute | solution.py:52
  188.2 10.1 %collective-permute-done.15 = bf16[200,1024]{1,0:T(8,128)(2,1)S(1)} collective-permute-done((bf16[200,1024]{1,0:T(8,128)(2,1)S(1)}, bf16[200,1024]{1,0:T(8,128)(2,1)S(1)}, u32[]{:S(2)}, u32[]{:S(2)}) %collective-permute-start.15) | collective-permute-done | bytes 409632 | tf_op jit(solution)/shard_map/ppermute | solution.py:52
  199.0 10.2 %collective-permute-done.16 = bf16[200,1024]{1,0:T(8,128)(2,1)} collective-permute-done((bf16[200,1024]{1,0:T(8,128)(2,1)S(1)}, bf16[200,1024]{1,0:T(8,128)(2,1)}, u32[]{:S(2)}, u32[]{:S(2)}) %collective-permute-start.16) | collective-permute-done | bytes 409632 | tf_op jit(solution)/shard_map/ppermute | solution.py:52
  209.2 7.6 %collective-permute-start.1 = (bf16[1,1600]{1,0:T(2,128)(2,1)S(1)}, bf16[1,1600]{1,0:T(2,128)(2,1)S(1)}, u32[]{:S(2)}, u32[]{:S(2)}) collective-permute-start(bf16[1,1600]{1,0:T(2,128)(2,1)S(1)} %reshape.96), channel_id=1, source_target_pairs={{1,0},{0,1},{3,2},{2,3},{5,4},{4,5},{7,6},{6,7},{9,8},{8,9},{11,10... | collective-permute-start | bytes 9608 | tf_op jit(solution)/shard_map/ppermute | solution.py:19
  216.9 9.1 %collective-permute-start.3 = (s32[128]{0:T(128)S(1)}, s32[128]{0:T(128)S(1)}, u32[]{:S(2)}, u32[]{:S(2)}) collective-permute-start(s32[128]{0:T(128)S(1)} %dynamic_slice.14), channel_id=1, source_target_pairs={{0,2},{2,0},{4,6},{6,4},{8,10},{10,8},{12,14},{14,12},{16,18},{18,... | collective-permute-start | bytes 1544 | tf_op jit(solution)/shard_map/ppermute | solution.py:14
  243.3 7.3 %collective-permute-done.20 = bf16[200,1024]{1,0:T(8,128)(2,1)S(1)} collective-permute-done((bf16[200,1024]{1,0:T(8,128)(2,1)}, bf16[200,1024]{1,0:T(8,128)(2,1)S(1)}, u32[]{:S(2)}, u32[]{:S(2)}) %collective-permute-start.20) | collective-permute-done | bytes 409632 | tf_op jit(solution)/shard_map/ppermute | solution.py:52
  282.5 14.3 %fusion.9 = f32[512,3072]{1,0:T(8,128)S(1)} fusion(bf16[3200,3072]{1,0:T(8,128)(2,1)} %all-gather.2.cloned.1.call-done, bf16[512,3200]{0,1:T(8,128)(2,1)S(1)} %constant_dynamic-update-slice_fusion.32, f32[3200]{0:T(1024)S(1)} %mul.109, f32[512]{0:T(512)S(1)} %add_rsqrt_fusion.2), kind=kOutput, calls=%fused_computation.15 | convolution fusion | flops 10072883200 | bytes 29243904 | tf_op jit(solution)/shard_map/dot_general | solution.py:62
  299.8 8.9 %collective-permute-start.2 = (bf16[128,1024]{1,0:T(8,128)(2,1)S(1)}, bf16[128,1024]{1,0:T(8,128)(2,1)}, u32[]{:S(2)}, u32[]{:S(2)}) collective-permute-start(bf16[128,1024]{1,0:T(8,128)(2,1)S(1)} %constant_dynamic-slice_fusion.1), channel_id=1, source_target_pairs={{0,2},{2,0},{4,6},{6,4},{8,10},{10,8},{12,14},{14,12},{16,18},{18,... | collective-permute-start | bytes 786440 | tf_op jit(solution)/shard_map/ppermute | solution.py:14
  308.7 9.8 %all-reduce = (f32[512]{0:T(512)S(1)}, f32[512]{0:T(512)S(1)}) all-reduce(f32[512]{0:T(512)S(1)} %get-tuple-element.10, f32[512]{0:T(512)S(1)} %get-tuple-element.9), channel_id=1, replica_groups=mesh['group'=16,'tp'=2] {'tp'}, use_global_device_ids=true, to_apply=%region_7.8 | all-reduce | flops 1024 | bytes 8192 | tf_op jit(solution)/shard_map/psum | solution.py:66
  327.1 6.8 %fusion.26 = f32[8,512,640]{2,1,0:T(8,128)} fusion(bf16[64,8,8,128]{3,2,1,0:T(8,128)(2,1)} %get-tuple-element.13, bf16[128,1024]{1,0:T(8,128)(2,1)} %collective-permute-done.4, bf16[512,1024]{1,0:T(8,128)(2,1)S(1)} %get-tuple-element.14), kind=kOutput, calls=%fused_computation.32 | convolution fusion | flops 673710080 | bytes 12845056 | tf_op jit(solution)/shard_map/qhd,khd->hqk/dot_general | solution.py:85
  333.9 15.5 %fusion.45 = (f32[8,512]{1,0:T(8,128)S(1)}, f32[8,512,640]{2,1,0:T(8,128)}) fusion(f32[8,512,640]{2,1,0:T(8,128)} %fusion.26, pred[512,640]{1,0:T(8,128)(4,1)} %broadcast_compare_fusion), kind=kOutput, calls=%fused_computation.97 | output fusion | flops 15729279 | bytes 21315584 | tf_op jit(solution)/shard_map/sub | solution.py:91
  349.5 6.1 %fusion.25 = bf16[8,128,512]{2,1,0:T(8,128)(2,1)S(1)} fusion(bf16[640,8,128]{0,2,1:T(8,128)(2,1)S(1)} %bitcast.51, f32[8,512,640]{2,1,0:T(8,128)} %get-tuple-element.18, f32[8,512]{1,0:T(8,128)S(1)} %get-tuple-element.17), kind=kOutput, calls=%fused_computation.31 | convolution fusion | flops 676855808 | bytes 12861440 | tf_op jit(solution)/shard_map/hqk,khd->qhd/dot_general | solution.py:96
  367.1 13.9 %collective-permute-done.21 = bf16[512,1024]{0,1:T(8,128)(2,1)} collective-permute-done((bf16[512,1024]{0,1:T(8,128)(2,1)S(1)}, bf16[512,1024]{0,1:T(8,128)(2,1)}, u32[]{:S(2)}, u32[]{:S(2)}) %collective-permute-start.21) | collective-permute-done | bytes 1048608 | tf_op jit(solution)/shard_map/ppermute | solution.py:19
  381.0 8.7 %convolution_convert_fusion = bf16[1024,1600]{0,1:T(8,128)(2,1)} fusion(s32[512]{0:T(512)S(1)} %multiply_add_fusion, bf16[512,1600]{0,1:T(8,128)(2,1)} %fusion.17, bf16[512,1600]{0,1:T(8,128)(2,1)S(1)} %copy-done.30, bf16[512,1024]{0,1:T(8,128)(2,1)} %collective-permute-done.21, bf16[6400,1024]{1,0:T(8,128)(2,1)} %constant_dynamic-update-slice_fusion, ...), kind=kOutput, calls=%fused_computation.14 | convolution fusion | flops 3364159488 | bytes 10887428 | tf_op jit(solution)/shard_map/dot_general | solution.py:117
  394.1 79.9 %all_to_all.5 = bf16[16,64,1600]{2,1,0:T(8,128)(2,1)S(1)} all-to-all(bf16[16,64,1600]{2,1,0:T(8,128)(2,1)S(1)} %bitcast.48), channel_id=1, replica_groups=mesh['group'=16,'tp'=2] {'group'}, dimensions={0} | all-to-all | bytes 6553600 | tf_op jit(solution)/shard_map/all_to_all | solution.py:119
  (170 shorter events, 101.6 us)
Async XLA Ops:
  6.5 221.0 %copy-start.35 = (f32[2,1024]{1,0:T(2,128)S(1)}, f32[2,1024]{1,0:T(2,128)}, u32[]{:S(2)}) copy-start(f32[2,1024]{1,0:T(2,128)} %param.11) | copy-start | bytes 24580
  6.5 275.9 %all-gather.2.cloned.1.call-start = ((), (), s32[]{:S(2)}) async-start(), calls=%async_computation.1 | async-start | bytes 20889600 | tf_op jit(solution)/shard_map/all_gather | solution.py:29
  9.0 38.0 %collective-permute-start = (bf16[512,1600]{0,1:T(8,128)(2,1)}, bf16[512,1600]{0,1:T(8,128)(2,1)}, u32[]{:S(2)}, u32[]{:S(2)}) collective-permute-start(bf16[512,1600]{0,1:T(8,128)(2,1)} %param.8), channel_id=1, source_target_pairs={{1,0},{0,1},{3,2},{2,3},{5,4},{4,5},{7,6},{6,7},{9,8},{8,9},{11,10... | collective-permute-start | bytes 4915208 | tf_op jit(solution)/shard_map/ppermute | solution.py:19
  48.6 1.7 collective-permute-start.5
  51.0 16.3 %collective-permute-start.6 = (bf16[200,1024]{1,0:T(8,128)(2,1)S(1)}, bf16[200,1024]{1,0:T(8,128)(2,1)S(1)}, u32[]{:S(2)}, u32[]{:S(2)}) collective-permute-start(bf16[200,1024]{1,0:T(8,128)(2,1)S(1)} %collective-permute-done.5), channel_id=1, source_target_pairs={{0,2},{2,4},{4,6},{6,8},{8,10},{10,12},{12,14},{14,16},{16,18},{18... | collective-permute-start | bytes 1228808 | tf_op jit(solution)/shard_map/ppermute | solution.py:52
  68.0 34.9 %collective-permute-start.7 = (bf16[200,1024]{1,0:T(8,128)(2,1)S(1)}, bf16[200,1024]{1,0:T(8,128)(2,1)S(1)}, u32[]{:S(2)}, u32[]{:S(2)}) collective-permute-start(bf16[200,1024]{1,0:T(8,128)(2,1)S(1)} %collective-permute-done.6), channel_id=1, source_target_pairs={{0,2},{2,4},{4,6},{6,8},{8,10},{10,12},{12,14},{14,16},{16,18},{18... | collective-permute-start | bytes 1228808 | tf_op jit(solution)/shard_map/ppermute | solution.py:52
  103.7 18.6 %collective-permute-start.8 = (bf16[200,1024]{1,0:T(8,128)(2,1)S(1)}, bf16[200,1024]{1,0:T(8,128)(2,1)S(1)}, u32[]{:S(2)}, u32[]{:S(2)}) collective-permute-start(bf16[200,1024]{1,0:T(8,128)(2,1)S(1)} %collective-permute-done.7), channel_id=1, source_target_pairs={{0,2},{2,4},{4,6},{6,8},{8,10},{10,12},{12,14},{14,16},{16,18},{18... | collective-permute-start | bytes 1228808 | tf_op jit(solution)/shard_map/ppermute | solution.py:52
  123.1 10.1 %collective-permute-start.9 = (bf16[200,1024]{1,0:T(8,128)(2,1)S(1)}, bf16[200,1024]{1,0:T(8,128)(2,1)S(1)}, u32[]{:S(2)}, u32[]{:S(2)}) collective-permute-start(bf16[200,1024]{1,0:T(8,128)(2,1)S(1)} %collective-permute-done.8), channel_id=1, source_target_pairs={{0,2},{2,4},{4,6},{6,8},{8,10},{10,12},{12,14},{14,16},{16,18},{18... | collective-permute-start | bytes 1228808 | tf_op jit(solution)/shard_map/ppermute | solution.py:52
  134.0 10.1 %collective-permute-start.10 = (bf16[200,1024]{1,0:T(8,128)(2,1)S(1)}, bf16[200,1024]{1,0:T(8,128)(2,1)S(1)}, u32[]{:S(2)}, u32[]{:S(2)}) collective-permute-start(bf16[200,1024]{1,0:T(8,128)(2,1)S(1)} %collective-permute-done.9), channel_id=1, source_target_pairs={{0,2},{2,4},{4,6},{6,8},{8,10},{10,12},{12,14},{14,16},{16,18},{18... | collective-permute-start | bytes 1228808 | tf_op jit(solution)/shard_map/ppermute | solution.py:52
  144.8 10.1 %collective-permute-start.11 = (bf16[200,1024]{1,0:T(8,128)(2,1)S(1)}, bf16[200,1024]{1,0:T(8,128)(2,1)S(1)}, u32[]{:S(2)}, u32[]{:S(2)}) collective-permute-start(bf16[200,1024]{1,0:T(8,128)(2,1)S(1)} %collective-permute-done.10), channel_id=1, source_target_pairs={{0,2},{2,4},{4,6},{6,8},{8,10},{10,12},{12,14},{14,16},{16,18},{18... | collective-permute-start | bytes 1228808 | tf_op jit(solution)/shard_map/ppermute | solution.py:52
  155.6 10.1 %collective-permute-start.12 = (bf16[200,1024]{1,0:T(8,128)(2,1)S(1)}, bf16[200,1024]{1,0:T(8,128)(2,1)S(1)}, u32[]{:S(2)}, u32[]{:S(2)}) collective-permute-start(bf16[200,1024]{1,0:T(8,128)(2,1)S(1)} %collective-permute-done.11), channel_id=1, source_target_pairs={{0,2},{2,4},{4,6},{6,8},{8,10},{10,12},{12,14},{14,16},{16,18},{18... | collective-permute-start | bytes 1228808 | tf_op jit(solution)/shard_map/ppermute | solution.py:52
  166.5 10.1 %collective-permute-start.13 = (bf16[200,1024]{1,0:T(8,128)(2,1)S(1)}, bf16[200,1024]{1,0:T(8,128)(2,1)S(1)}, u32[]{:S(2)}, u32[]{:S(2)}) collective-permute-start(bf16[200,1024]{1,0:T(8,128)(2,1)S(1)} %collective-permute-done.12), channel_id=1, source_target_pairs={{0,2},{2,4},{4,6},{6,8},{8,10},{10,12},{12,14},{14,16},{16,18},{18... | collective-permute-start | bytes 1228808 | tf_op jit(solution)/shard_map/ppermute | solution.py:52
  177.3 10.1 %collective-permute-start.14 = (bf16[200,1024]{1,0:T(8,128)(2,1)S(1)}, bf16[200,1024]{1,0:T(8,128)(2,1)S(1)}, u32[]{:S(2)}, u32[]{:S(2)}) collective-permute-start(bf16[200,1024]{1,0:T(8,128)(2,1)S(1)} %collective-permute-done.13), channel_id=1, source_target_pairs={{0,2},{2,4},{4,6},{6,8},{8,10},{10,12},{12,14},{14,16},{16,18},{18... | collective-permute-start | bytes 1228808 | tf_op jit(solution)/shard_map/ppermute | solution.py:52
  188.2 10.1 %collective-permute-start.15 = (bf16[200,1024]{1,0:T(8,128)(2,1)S(1)}, bf16[200,1024]{1,0:T(8,128)(2,1)S(1)}, u32[]{:S(2)}, u32[]{:S(2)}) collective-permute-start(bf16[200,1024]{1,0:T(8,128)(2,1)S(1)} %collective-permute-done.14), channel_id=1, source_target_pairs={{0,2},{2,4},{4,6},{6,8},{8,10},{10,12},{12,14},{14,16},{16,18},{18... | collective-permute-start | bytes 1228808 | tf_op jit(solution)/shard_map/ppermute | solution.py:52
  199.0 10.2 %collective-permute-start.16 = (bf16[200,1024]{1,0:T(8,128)(2,1)S(1)}, bf16[200,1024]{1,0:T(8,128)(2,1)}, u32[]{:S(2)}, u32[]{:S(2)}) collective-permute-start(bf16[200,1024]{1,0:T(8,128)(2,1)S(1)} %collective-permute-done.15), channel_id=1, source_target_pairs={{0,2},{2,4},{4,6},{6,8},{8,10},{10,12},{12,14},{14,16},{16,18},{18... | collective-permute-start | bytes 1228808 | tf_op jit(solution)/shard_map/ppermute | solution.py:52
  209.2 17.9 %collective-permute-start.17 = (bf16[200,1024]{1,0:T(8,128)(2,1)}, bf16[200,1024]{1,0:T(8,128)(2,1)}, u32[]{:S(2)}, u32[]{:S(2)}) collective-permute-start(bf16[200,1024]{1,0:T(8,128)(2,1)} %collective-permute-done.16), channel_id=1, source_target_pairs={{0,2},{2,4},{4,6},{6,8},{8,10},{10,12},{12,14},{14,16},{16,18},{18... | collective-permute-start | bytes 1228808 | tf_op jit(solution)/shard_map/ppermute | solution.py:52
  209.2 26.9 %collective-permute-start.1 = (bf16[1,1600]{1,0:T(2,128)(2,1)S(1)}, bf16[1,1600]{1,0:T(2,128)(2,1)S(1)}, u32[]{:S(2)}, u32[]{:S(2)}) collective-permute-start(bf16[1,1600]{1,0:T(2,128)(2,1)S(1)} %reshape.96), channel_id=1, source_target_pairs={{1,0},{0,1},{3,2},{2,3},{5,4},{4,5},{7,6},{6,7},{9,8},{8,9},{11,10... | collective-permute-start | bytes 9608 | tf_op jit(solution)/shard_map/ppermute | solution.py:19
  216.9 18.2 %collective-permute-start.3 = (s32[128]{0:T(128)S(1)}, s32[128]{0:T(128)S(1)}, u32[]{:S(2)}, u32[]{:S(2)}) collective-permute-start(s32[128]{0:T(128)S(1)} %dynamic_slice.14), channel_id=1, source_target_pairs={{0,2},{2,0},{4,6},{6,4},{8,10},{10,8},{12,14},{14,12},{16,18},{18,... | collective-permute-start | bytes 1544 | tf_op jit(solution)/shard_map/ppermute | solution.py:14
  227.1 5.3 %collective-permute-start.18 = (bf16[200,1024]{1,0:T(8,128)(2,1)}, bf16[200,1024]{1,0:T(8,128)(2,1)}, u32[]{:S(2)}, u32[]{:S(2)}) collective-permute-start(bf16[200,1024]{1,0:T(8,128)(2,1)} %collective-permute-done.17), channel_id=1, source_target_pairs={{0,2},{2,4},{4,6},{6,8},{8,10},{10,12},{12,14},{14,16},{16,18},{18... | collective-permute-start | bytes 1228808 | tf_op jit(solution)/shard_map/ppermute | solution.py:52
  232.4 8.0 %collective-permute-start.19 = (bf16[200,1024]{1,0:T(8,128)(2,1)}, bf16[200,1024]{1,0:T(8,128)(2,1)}, u32[]{:S(2)}, u32[]{:S(2)}) collective-permute-start(bf16[200,1024]{1,0:T(8,128)(2,1)} %collective-permute-done.18), channel_id=1, source_target_pairs={{0,2},{2,4},{4,6},{6,8},{8,10},{10,12},{12,14},{14,16},{16,18},{18... | collective-permute-start | bytes 1228808 | tf_op jit(solution)/shard_map/ppermute | solution.py:52
  240.4 10.3 %collective-permute-start.20 = (bf16[200,1024]{1,0:T(8,128)(2,1)}, bf16[200,1024]{1,0:T(8,128)(2,1)S(1)}, u32[]{:S(2)}, u32[]{:S(2)}) collective-permute-start(bf16[200,1024]{1,0:T(8,128)(2,1)} %collective-permute-done.19), channel_id=1, source_target_pairs={{0,2},{2,4},{4,6},{6,8},{8,10},{10,12},{12,14},{14,16},{16,18},{18... | collective-permute-start | bytes 1228808 | tf_op jit(solution)/shard_map/ppermute | solution.py:52
  299.8 24.7 %collective-permute-start.2 = (bf16[128,1024]{1,0:T(8,128)(2,1)S(1)}, bf16[128,1024]{1,0:T(8,128)(2,1)}, u32[]{:S(2)}, u32[]{:S(2)}) collective-permute-start(bf16[128,1024]{1,0:T(8,128)(2,1)S(1)} %constant_dynamic-slice_fusion.1), channel_id=1, source_target_pairs={{0,2},{2,0},{4,6},{6,4},{8,10},{10,8},{12,14},{14,12},{16,18},{18,... | collective-permute-start | bytes 786440 | tf_op jit(solution)/shard_map/ppermute | solution.py:14
  322.9 4.2 collective-permute-start.4
  355.5 25.5 %collective-permute-start.21 = (bf16[512,1024]{0,1:T(8,128)(2,1)S(1)}, bf16[512,1024]{0,1:T(8,128)(2,1)}, u32[]{:S(2)}, u32[]{:S(2)}) collective-permute-start(bf16[512,1024]{0,1:T(8,128)(2,1)S(1)} %bitcast.58), channel_id=1, source_target_pairs={{1,0},{0,1},{3,2},{2,3},{5,4},{4,5},{7,6},{6,7},{9,8},{8,9},{11,10... | collective-permute-start | bytes 3145736 | tf_op jit(solution)/shard_map/ppermute | solution.py:19
  (36 other events, 1187.5 us)
Sparse Core Ops, SparseCore 0:
  9.1 114.0 all-gather.1
